TPU v7x, 32 devices: a whole 2x2x4 slice. The times are simulated.
32 devices in a mesh: dp: 8 (over z, x), outer: 4 (over y, core).
Axes of the slice: x: 2, y: 2, z: 4, core: 2. Of those that a mesh axis runs over, the one named last changes fastest.
Arguments:
- partials: bfloat16 [4, 8, 2, 16, 8192], P('outer', 'dp'), may hold values from -3500 to 3500, as said below
- master: float32 [2, 16, 8192], P(None, 'dp'), may hold values from -6 to 6
- m_codes: bfloat16 [2, 16, 8192], P(None, 'dp'), may hold values from -1 to 1
- v_codes: bfloat16 [2, 16, 8192], P(None, 'dp'), may hold values from 0.049804688 to 1
- m_scales: float32 [2, 16, 4], P(None, 'dp'), may hold values from 0.0001 to 0.001
- v_scales: float32 [2, 16, 4], P(None, 'dp'), may hold values from 1e-08 to 1e-07
Outputs:
- new_master: float32 [2, 16, 8192], P(None, 'dp')
- new_m_codes: bfloat16 [2, 16, 8192], P(None, 'dp')
- new_v_codes: bfloat16 [2, 16, 8192], P(None, 'dp')
- new_m_scales: float32 [2, 16, 4], P(None, 'dp')
- new_v_scales: float32 [2, 16, 4], P(None, 'dp')
- weights: bfloat16 [2, 16, 8192], replicated
Inputs may be any that keep to these rules, and one draw needn't show every extreme that they name: Gradient partials of real values; entries vary from row to row and column to column.
All inputs are finite; a program needn't handle non-finite values. Where the computation divides by a largest or mean magnitude, that divisor is 1e-20 or more.
Results may differ from a plain program's by a relative error of at most 0.0004.
Values may be sent and summed in bfloat16 or wider, within the bound.
No kernel may reach another device: no remote copies, remote signals or barrier semaphores. Data moves between devices by JAX's collectives and lax.ppermute only.
A program may use at most 64 MiB of HBM per device.

v0:
```python
import jax
import jax.numpy as jnp
from jax import lax
from jax.sharding import PartitionSpec as P

BLOCK = 2048
STEP = 10


def adam_blocks(gradient, master, m_codes, v_codes, m_scales, v_scales, clip_factor):
    count = gradient.shape[0]
    rows = gradient.shape[1]
    blocks = gradient.shape[2] // BLOCK
    shape_four = (count, rows, blocks, BLOCK)
    moment = m_codes.astype(jnp.float32).reshape(shape_four) * m_scales[..., None]
    second = v_codes.astype(jnp.float32).reshape(shape_four) * v_scales[..., None]
    scaled = clip_factor * gradient.reshape(shape_four)
    moment = 0.9 * moment + 0.1 * scaled
    second = 0.95 * second + 0.05 * scaled * scaled
    update = moment / (1.0 - 0.9**STEP) / (jnp.sqrt(second / (1.0 - 0.95**STEP)) + 1e-08)
    fresh = master - 0.01 * update.reshape(master.shape)
    m_top = jnp.max(jnp.abs(moment), axis=3) + 1e-20
    v_top = jnp.max(jnp.abs(second), axis=3) + 1e-20
    m_next = (moment / m_top[..., None]).astype(jnp.bfloat16).reshape(master.shape)
    v_next = (second / v_top[..., None]).astype(jnp.bfloat16).reshape(master.shape)
    return (fresh, m_next, v_next, m_top, v_top, fresh.astype(jnp.bfloat16))


def body(partials, master, m_codes, v_codes, m_scales, v_scales):
    own_terms = partials[0, 0]
    row_part = lax.psum_scatter(
        own_terms.astype(jnp.float32), "dp", scatter_dimension=1, tiled=True
    )
    gradient = lax.psum(row_part, "outer")
    total = lax.psum(jnp.sum(gradient * gradient), "dp")
    clip_factor = 1.0 / jnp.maximum(jnp.sqrt(total), 1.0)
    results = adam_blocks(gradient, master, m_codes, v_codes, m_scales, v_scales, clip_factor)
    fresh, m_next, v_next, m_top, v_top, rounded = results
    weights = lax.all_gather(rounded, "dp", axis=1, tiled=True)
    return (fresh, m_next, v_next, m_top, v_top, weights)


def solution(mesh):
    return jax.shard_map(
        body,
        mesh=mesh,
        in_specs=(
            P("outer", "dp", None, None, None),
            P(None, "dp", None),
            P(None, "dp", None),
            P(None, "dp", None),
            P(None, "dp", None),
            P(None, "dp", None),
        ),
        out_specs=(
            P(None, "dp", None),
            P(None, "dp", None),
            P(None, "dp", None),
            P(None, "dp", None),
            P(None, "dp", None),
            P(),
        ),
        check_vma=False,
    )
```

profile of v0, /device:TPU:0, one launch (start us, length us, event | category | flops | bytes accessed | tf_op | source)
XLA Modules:
  0.0 194.2 jit_solution(15518864114638072132)
XLA Ops:
  7.2 0.0 all-reduce.6.cloned.1.call-start
  7.2 2.1 %bitcast_convert_fusion = f32[2,16,8192]{2,1,0:T(8,128)} fusion(bf16[1,1,2,16,8192]{4,3,2,1,0:T(8,128)(2,1)} %param.6), kind=kLoop, calls=%fused_computation | loop fusion | flops 262144 | bytes 1572864 | tf_op jit(solution)/shard_map/convert_element_type | solution.py:32
  9.3 0.0 all-reduce.6.cloned.1.call-update
  9.4 0.0 all-reduce.4.cloned.1.call-start
  9.4 0.0 copy-start.8
  9.4 0.6 copy-done.8
  10.1 0.6 dynamic-slice
  11.3 81.3 %all-reduce.6.cloned.1.call-done = f32[2,16,8192]{2,1,0:T(8,128)} async-done(((f32[2,16,8192]{2,1,0:T(8,128)}), f32[2,16,8192]{2,1,0:T(8,128)}) %all-reduce.6.cloned.1.call-update) | async-done | bytes 1048592
  92.6 1.7 constant_dynamic-slice_fusion
  94.3 0.0 copy-start.5
  94.3 0.0 all-reduce.4.cloned.1.call-update
  94.4 0.7 copy-done.5
  95.0 0.1 mul.104
  95.1 0.0 copy-start.4
  95.1 0.1 mul.105
  95.3 0.5 copy-done.4
  95.8 0.1 mul.114
  95.9 0.0 copy-start.1
  95.9 0.1 mul.115
  96.0 0.7 copy-done.1
  96.7 0.1 reshape.40
  96.8 0.0 copy-start
  96.8 30.1 %all-reduce.4.cloned.1.call-done = f32[2,2,8192]{2,1,0:T(2,128)} async-done(((f32[2,2,8192]{2,1,0:T(2,128)}), f32[2,2,8192]{2,1,0:T(2,128)}) %all-reduce.4.cloned.1.call-update) | async-done | bytes 131088 | tf_op jit(solution)/shard_map/psum | solution.py:34
  126.9 0.0 copy-start.3
  126.9 1.7 multiply_reduce_fusion
  128.6 0.0 copy-done
  128.6 0.0 copy-start.2
  128.6 0.1 reshape.41
  128.6 22.0 %psum.15 = f32[]{:T(128)} all-reduce(f32[]{:T(128)} %multiply_reduce_fusion), channel_id=1, replica_groups=mesh['dp'=8,'outer'=4] {'dp'}, use_global_device_ids=true, to_apply=%region_3.0 | all-reduce | flops 1 | bytes 8 | tf_op jit(solution)/shard_map/psum | solution.py:35
  151.4 0.0 copy-done.3
  151.4 0.0 copy-done.2
  151.4 1.1 fusion.4
  152.5 0.1 mul.127
  152.6 0.3 fusion.3
  152.9 0.0 copy-start.7
  152.9 0.0 copy-start.6
  152.9 0.1 div.47
  153.0 0.5 copy-done.7
  153.5 0.1 div.48
  153.6 0.0 copy-done.6
  153.6 0.1 div.50
  153.7 0.1 div.51
  153.9 0.1 copy.12
  153.9 31.4 %all_gather.3 = bf16[2,16,8192]{2,0,1:T(2,128)(2,1)S(1)} all-gather(bf16[2,2,8192]{2,0,1:T(2,128)(2,1)S(1)} %copy.12), channel_id=1, replica_groups=mesh['dp'=8,'outer'=4] {'dp'}, dimensions={1}, use_global_device_ids=true | all-gather | bytes 589824 | tf_op jit(solution)/shard_map/all_gather | solution.py:39
  185.3 1.1 copy.13
  186.4 1.0 divide_convert_fusion
  (1 shorter events, 0.0 us)
Async XLA Ops:
  7.2 85.4 %all-reduce.6.cloned.1.call-start = ((), (), s32[]{:S(2)}) async-start(), calls=%async_computation.1 | async-start | bytes 2097152
  9.4 117.5 %all-reduce.4.cloned.1.call-start = ((), (), s32[]{:S(2)}) async-start(), calls=%async_computation | async-start | bytes 262144 | tf_op jit(solution)/shard_map/psum | solution.py:34
  9.4 0.7 copy-start.8
  94.3 0.7 copy-start.5
  95.1 0.7 copy-start.4
  95.9 0.8 copy-start.1
  96.8 31.8 %copy-start = (bf16[2,2,8192]{2,1,0:T(2,128)(2,1)S(1)}, bf16[2,2,8192]{2,1,0:T(2,128)(2,1)}, u32[]{:S(2)}) copy-start(bf16[2,2,8192]{2,1,0:T(2,128)(2,1)} %param.9) | copy-start | bytes 196612
  126.9 24.5 %copy-start.3 = (f32[2,2,8192]{2,1,0:T(2,128)S(1)}, f32[2,2,8192]{2,1,0:T(2,128)}, u32[]{:S(2)}) copy-start(f32[2,2,8192]{2,1,0:T(2,128)} %param.7) | copy-start | bytes 393220
  128.6 22.8 %copy-start.2 = (f32[2,2,8192]{2,1,0:T(2,128)S(1)}, f32[2,2,8192]{2,1,0:T(2,128)}, u32[]{:S(2)}) copy-start(f32[2,2,8192]{2,1,0:T(2,128)} %all-reduce.4.cloned.1.call-done) | copy-start | bytes 393220
  152.9 0.6 copy-start.7
  152.9 0.7 copy-start.6
Sparse Core Ops, SparseCore 0:
  11.5 81.0 all-reduce.5
  95.5 31.3 all-reduce.3
where the time goes:
time: 195 us; the launch traced here: 194 us
  waiting for transfers between devices  111 us (57%)
  blocking collectives  53.4 us (27%)
  between operations  15.6 us (8%)
  local copies, waits for them, and re-layouts  7.63 us (4%)
  other arithmetic  6.17 us (3%)
    unnamed x3, waiting for transfers between devices  81.3 us
    all_gather x1, blocking collectives, body(): weights = lax.all_gather(rounded, 'dp', axis=1, tiled=True)  31.4 us
    psum x1, waiting for transfers between devices, body(): gradient = lax.psum(row_part, 'outer')  30.1 us
    psum x1, blocking collectives, body(): total = lax.psum(jnp.sum(gradient * gradient), 'dp')  22 us
    unnamed x21, local copies, waits for them, and re-layouts  6.46 us
  transfers between devices with their start and end apart: 2, of which 2 were waited for; matrix products, arithmetic and copies ran while one was open for 1% of the time, Pallas kernels for 0%

commit v1 on v0

--- a/solution.py
+++ b/solution.py
@@ -31,7 +31,7 @@
     row_part = lax.psum_scatter(
         own_terms.astype(jnp.float32), "dp", scatter_dimension=1, tiled=True
     )
-    gradient = lax.psum(row_part, "outer")
+    gradient = jnp.sum(lax.all_gather(row_part, "outer"), axis=0)
     total = lax.psum(jnp.sum(gradient * gradient), "dp")
     clip_factor = 1.0 / jnp.maximum(jnp.sqrt(total), 1.0)
     results = adam_blocks(gradient, master, m_codes, v_codes, m_scales, v_scales, clip_factor)

time: 195 us -> 167 us (0.86)
  waiting for transfers between devices: 111 us -> 78.8 us
  blocking collectives: 53.4 us -> 59 us
    psum x1 -> x0, waiting for transfers between devices: 30.1 us -> none  [body(): gradient = lax.psum(row_part, 'outer')]
    all_gather x0 -> x1, blocking collectives: none -> 7.15 us  [body(): gradient = jnp.sum(lax.all_gather(row_part, 'outer'), axis=0)]
    unnamed x3 -> x2, waiting for transfers between devices: 81.3 us -> 78.8 us
  transfers between devices with their start and end apart: 2 -> 1, of which waited for: 2 -> 1; matrix products, arithmetic and copies ran while one was open for 1% -> 1% of each run, Pallas kernels for 0% -> 0%
where the time goes in v1:
time: 167 us
  waiting for transfers between devices  78.8 us (47%)
  blocking collectives  59 us (35%)
  between operations  15.6 us (9%)
  local copies, waits for them, and re-layouts  7.58 us (5%)
  other arithmetic  5.72 us (3%)
    unnamed x2, waiting for transfers between devices  78.8 us
    all_gather x1, blocking collectives, body(): weights = lax.all_gather(rounded, 'dp', axis=1, tiled=True)  31.2 us
    psum x1, blocking collectives, body(): total = lax.psum(jnp.sum(gradient * gradient), 'dp')  20.7 us
    all_gather x1, blocking collectives, body(): gradient = jnp.sum(lax.all_gather(row_part, 'outer'), axis=0)  7.15 us
    unnamed x21, local copies, waits for them, and re-layouts  6.4 us
  transfers between devices with their start and end apart: 1, of which 1 were waited for; matrix products, arithmetic and copies ran while one was open for 1% of the time, Pallas kernels for 0%

profile of v1, /device:TPU:0, one launch (start us, length us, event | category | flops | bytes accessed | tf_op | source)
XLA Modules:
  0.0 166.7 jit_solution(9270559959030567855)
XLA Ops:
  7.2 0.0 all-reduce.3.cloned.1.call-start
  7.2 2.1 %bitcast_convert_fusion = f32[2,16,8192]{2,1,0:T(8,128)} fusion(bf16[1,1,2,16,8192]{4,3,2,1,0:T(8,128)(2,1)} %param.6), kind=kLoop, calls=%fused_computation | loop fusion | flops 262144 | bytes 1572864 | tf_op jit(solution)/shard_map/convert_element_type | solution.py:32
  9.4 0.0 all-reduce.3.cloned.1.call-update
  9.4 0.0 copy-start.5
  9.4 0.7 copy-done.5
  10.1 0.1 mul.104
  10.2 0.0 copy-start.6
  10.2 0.1 reshape.47
  10.3 0.5 copy-done.6
  10.9 0.1 mul.114
  10.9 0.0 copy-start.1
  11.0 0.1 reshape.48
  11.1 0.7 copy-done.1
  11.8 0.1 reshape.40
  11.9 0.0 copy-start.7
  11.9 0.6 copy-done.7
  12.5 0.6 dynamic-slice
  13.7 78.7 %all-reduce.3.cloned.1.call-done = f32[2,16,8192]{2,1,0:T(8,128)} async-done(((f32[2,16,8192]{2,1,0:T(8,128)}), f32[2,16,8192]{2,1,0:T(8,128)}) %all-reduce.3.cloned.1.call-update) | async-done | bytes 1048592
  92.5 1.1 constant_dynamic-slice_fusion
  93.6 7.2 %all-gather = f32[8,2,8192]{2,1,0:T(2,128)S(1)} all-gather(f32[2,2,8192]{2,1,0:T(2,128)S(1)} %constant_dynamic-slice_fusion), channel_id=2, replica_groups=mesh['dp'=8,'outer'=4] {'outer'}, dimensions={0}, use_global_device_ids=true | all-gather | bytes 655360 | tf_op jit(solution)/shard_map/all_gather | solution.py:34
  100.7 0.3 reduce_sum.18
  101.0 0.0 copy-start
  101.0 0.7 multiply_reduce_fusion
  101.8 0.1 copy-done
  101.9 0.0 copy-start.2
  101.9 0.1 reshape.41
  101.9 20.7 %psum.7 = f32[]{:T(128)} all-reduce(f32[]{:T(128)} %multiply_reduce_fusion), channel_id=1, replica_groups=mesh['dp'=8,'outer'=4] {'dp'}, use_global_device_ids=true, to_apply=%region_3.0 | all-reduce | flops 1 | bytes 8 | tf_op jit(solution)/shard_map/psum | solution.py:35
  123.4 0.0 copy-done.2
  123.4 1.2 fusion.12
  124.6 0.1 mul.127
  124.7 0.3 fusion.3
  125.0 0.0 copy-start.3
  125.0 0.1 div.47
  125.1 0.5 copy-done.3
  125.6 0.1 div.48
  125.7 0.0 copy-start.4
  125.7 0.1 div.50
  125.8 0.5 copy-done.4
  126.3 0.1 div.51
  126.4 0.1 copy.34
  126.5 31.2 %all_gather.11 = bf16[2,16,8192]{2,0,1:T(2,128)(2,1)S(1)} all-gather(bf16[2,2,8192]{2,0,1:T(2,128)(2,1)S(1)} %copy.34), channel_id=1, replica_groups=mesh['dp'=8,'outer'=4] {'dp'}, dimensions={1}, use_global_device_ids=true | all-gather | bytes 589824 | tf_op jit(solution)/shard_map/all_gather | solution.py:39
  157.7 1.1 copy.37
  158.8 1.1 divide_convert_fusion
  (5 shorter events, 0.0 us)
Async XLA Ops:
  7.2 85.3 %all-reduce.3.cloned.1.call-start = ((), (), s32[]{:S(2)}) async-start(), calls=%async_computation | async-start | bytes 2097152
  9.4 0.7 copy-start.5
  10.2 0.7 copy-start.6
  10.9 0.8 copy-start.1
  11.9 0.7 copy-start.7
  101.0 0.8 copy-start
  101.9 21.5 %copy-start.2 = (f32[2,2,8192]{2,1,0:T(2,128)S(1)}, f32[2,2,8192]{2,1,0:T(2,128)}, u32[]{:S(2)}) copy-start(f32[2,2,8192]{2,1,0:T(2,128)} %param.7) | copy-start | bytes 393220
  125.0 0.6 copy-start.3
  125.7 0.6 copy-start.4
Sparse Core Ops, SparseCore 0:
  11.5 80.9 all-reduce.2

commit v2 on v0

--- a/solution.py
+++ b/solution.py
@@ -36,7 +36,9 @@
     clip_factor = 1.0 / jnp.maximum(jnp.sqrt(total), 1.0)
     results = adam_blocks(gradient, master, m_codes, v_codes, m_scales, v_scales, clip_factor)
     fresh, m_next, v_next, m_top, v_top, rounded = results
-    weights = lax.all_gather(rounded, "dp", axis=1, tiled=True)
+    weights = jnp.concatenate(
+        lax.all_to_all(jnp.stack([rounded] * lax.axis_size("dp")), "dp", 0, 0), axis=1
+    )
     return (fresh, m_next, v_next, m_top, v_top, weights)
 
 

time: 195 us -> 178 us (0.913)
  blocking collectives: 53.4 us -> 22 us
  waiting for transfers between devices: 111 us -> 121 us
  starting transfers between devices: 0.08 us -> 3.57 us
    all_gather x1 -> x0, blocking collectives: 31.4 us -> none  [body(): weights = lax.all_gather(rounded, 'dp', axis=1, tiled=True)]
    all_to_all x0 -> x1, waiting for transfers between devices: none -> 9.25 us  [body(): lax.all_to_all(jnp.stack([rounded] * lax.axis_size('dp')), 'dp', 0, 0)]
    all_to_all x0 -> x1, starting transfers between devices: none -> 3.49 us  [body(): lax.all_to_all(jnp.stack([rounded] * lax.axis_size('dp')), 'dp', 0, 0)]
  transfers between devices with their start and end apart: 2 -> 3, of which waited for: 2 -> 3; matrix products, arithmetic and copies ran while one was open for 1% -> 1% of each run, Pallas kernels for 0% -> 0%
where the time goes in v2:
time: 178 us; the launch traced here: 177 us
  waiting for transfers between devices  121 us (68%)
  blocking collectives  22 us (12%)
  between operations  15.6 us (9%)
  local copies, waits for them, and re-layouts  9.3 us (5%)
  other arithmetic  6.16 us (3%)
  starting transfers between devices  3.57 us (2%)
    unnamed x3, waiting for transfers between devices  81.3 us
    psum x1, waiting for transfers between devices, body(): gradient = lax.psum(row_part, 'outer')  30.1 us
    psum x1, blocking collectives, body(): total = lax.psum(jnp.sum(gradient * gradient), 'dp')  22 us
    all_to_all x1, waiting for transfers between devices, body(): lax.all_to_all(jnp.stack([rounded] * lax.axis_size('dp')), 'dp', 0, 0)  9.25 us
    unnamed x21, local copies, waits for them, and re-layouts  6.46 us
  transfers between devices with their start and end apart: 3, of which 3 were waited for; matrix products, arithmetic and copies ran while one was open for 1% of the time, Pallas kernels for 0%

profile of v2, /device:TPU:0, one launch (start us, length us, event | category | flops | bytes accessed | tf_op | source)
XLA Modules:
  0.0 177.2 jit_solution(13179929107595635660)
XLA Ops:
  7.2 0.0 all-reduce.6.cloned.1.call-start
  7.2 2.1 %bitcast_convert_fusion = f32[2,16,8192]{2,1,0:T(8,128)} fusion(bf16[1,1,2,16,8192]{4,3,2,1,0:T(8,128)(2,1)} %param.6), kind=kLoop, calls=%fused_computation | loop fusion | flops 262144 | bytes 1572864 | tf_op jit(solution)/shard_map/convert_element_type | solution.py:32
  9.3 0.0 all-reduce.6.cloned.1.call-update
  9.4 0.0 all-reduce.4.cloned.1.call-start
  9.4 0.0 copy-start.8
  9.4 0.6 copy-done.8
  10.1 0.6 dynamic-slice
  11.3 81.3 %all-reduce.6.cloned.1.call-done = f32[2,16,8192]{2,1,0:T(8,128)} async-done(((f32[2,16,8192]{2,1,0:T(8,128)}), f32[2,16,8192]{2,1,0:T(8,128)}) %all-reduce.6.cloned.1.call-update) | async-done | bytes 1048592
  92.6 1.7 constant_dynamic-slice_fusion
  94.3 0.0 copy-start.5
  94.3 0.0 all-reduce.4.cloned.1.call-update
  94.4 0.7 copy-done.5
  95.0 0.1 mul.104
  95.1 0.0 copy-start.4
  95.1 0.1 mul.105
  95.3 0.5 copy-done.4
  95.8 0.1 mul.114
  95.9 0.0 copy-start.1
  95.9 0.1 mul.115
  96.0 0.7 copy-done.1
  96.7 0.1 reshape.48
  96.8 0.0 copy-start
  96.8 30.1 %all-reduce.4.cloned.1.call-done = f32[2,2,8192]{2,1,0:T(2,128)} async-done(((f32[2,2,8192]{2,1,0:T(2,128)}), f32[2,2,8192]{2,1,0:T(2,128)}) %all-reduce.4.cloned.1.call-update) | async-done | bytes 131088 | tf_op jit(solution)/shard_map/psum | solution.py:34
  126.9 0.0 copy-start.3
  126.9 1.7 multiply_reduce_fusion
  128.6 0.0 copy-done
  128.6 0.0 copy-start.2
  128.6 0.1 reshape.49
  128.6 22.0 %psum.15 = f32[]{:T(128)} all-reduce(f32[]{:T(128)} %multiply_reduce_fusion), channel_id=1, replica_groups=mesh['dp'=8,'outer'=4] {'dp'}, use_global_device_ids=true, to_apply=%region_3.0 | all-reduce | flops 1 | bytes 8 | tf_op jit(solution)/shard_map/psum | solution.py:35
  151.4 0.0 copy-done.3
  151.4 0.0 copy-done.2
  151.4 1.1 fusion.4
  152.5 0.1 mul.127
  152.6 0.3 fusion.3
  152.9 0.0 copy-start.7
  152.9 0.0 copy-start.6
  152.9 0.1 div.47
  153.0 0.5 copy-done.7
  153.5 0.1 div.48
  153.6 0.0 copy-done.6
  153.6 0.1 div.50
  153.7 0.1 div.51
  153.9 1.2 stack.2
  155.1 3.5 %all-to-all-start = ((bf16[8,2,2,8192]{3,2,1,0:T(2,128)(2,1)}), bf16[8,2,2,8192]{3,2,1,0:T(2,128)(2,1)S(1)}, u32[]{:S(2)}, u32[]{:S(2)}) async-start(bf16[8,2,2,8192]{3,2,1,0:T(2,128)(2,1)} %stack.2), calls=%async_computation | async-start | bytes 1048576 | tf_op jit(solution)/shard_map/all_to_all | solution.py:40
  158.6 1.0 divide_convert_fusion
  159.5 9.2 %all-to-all-done = bf16[8,2,2,8192]{3,2,1,0:T(2,128)(2,1)S(1)} async-done(((bf16[8,2,2,8192]{3,2,1,0:T(2,128)(2,1)}), bf16[8,2,2,8192]{3,2,1,0:T(2,128)(2,1)S(1)}, u32[]{:S(2)}, u32[]{:S(2)}) %all-to-all-start) | async-done | bytes 524320 | tf_op jit(solution)/shard_map/all_to_all | solution.py:40
  168.8 0.5 copy.12
  169.3 1.1 copy.13
  (1 shorter events, 0.0 us)
Async XLA Ops:
  7.2 85.4 %all-reduce.6.cloned.1.call-start = ((), (), s32[]{:S(2)}) async-start(), calls=%async_computation.2 | async-start | bytes 2097152
  9.4 117.5 %all-reduce.4.cloned.1.call-start = ((), (), s32[]{:S(2)}) async-start(), calls=%async_computation.1 | async-start | bytes 262144 | tf_op jit(solution)/shard_map/psum | solution.py:34
  9.4 0.7 copy-start.8
  94.3 0.7 copy-start.5
  95.1 0.7 copy-start.4
  95.9 0.8 copy-start.1
  96.8 31.8 %copy-start = (bf16[2,2,8192]{2,1,0:T(2,128)(2,1)S(1)}, bf16[2,2,8192]{2,1,0:T(2,128)(2,1)}, u32[]{:S(2)}) copy-start(bf16[2,2,8192]{2,1,0:T(2,128)(2,1)} %param.9) | copy-start | bytes 196612
  126.9 24.5 %copy-start.3 = (f32[2,2,8192]{2,1,0:T(2,128)S(1)}, f32[2,2,8192]{2,1,0:T(2,128)}, u32[]{:S(2)}) copy-start(f32[2,2,8192]{2,1,0:T(2,128)} %param.7) | copy-start | bytes 393220
  128.6 22.8 %copy-start.2 = (f32[2,2,8192]{2,1,0:T(2,128)S(1)}, f32[2,2,8192]{2,1,0:T(2,128)}, u32[]{:S(2)}) copy-start(f32[2,2,8192]{2,1,0:T(2,128)} %all-reduce.4.cloned.1.call-done) | copy-start | bytes 393220
  152.9 0.6 copy-start.7
  152.9 0.7 copy-start.6
  155.1 13.7 %all-to-all-start = ((bf16[8,2,2,8192]{3,2,1,0:T(2,128)(2,1)}), bf16[8,2,2,8192]{3,2,1,0:T(2,128)(2,1)S(1)}, u32[]{:S(2)}, u32[]{:S(2)}) async-start(bf16[8,2,2,8192]{3,2,1,0:T(2,128)(2,1)} %stack.2), calls=%async_computation | async-start | bytes 1048576 | tf_op jit(solution)/shard_map/all_to_all | solution.py:40
Sparse Core Ops, SparseCore 0:
  11.5 81.0 all-reduce.5
  95.5 31.3 all-reduce.3
